TPU v7x, 512 devices: a whole 4x8x8 slice. The times are simulated.
512 devices in a mesh: req: 8 (over y), seq: 8 (over x, core), tp: 8 (over z).
Axes of the slice: x: 4, y: 8, z: 8, core: 2. Of those that a mesh axis runs over, the one named last changes fastest.
Arguments:
- tokens: bfloat16 [2048, 1024], P(('req', 'seq', 'tp')), may hold values from -3 to 3
- w_qkv: bfloat16 [1024, 3, 1024], P(None, None, 'tp'), may hold values from -0.1875 to 0.1875
- w_out: bfloat16 [1024, 1024], P('tp'), may hold values from -0.75 to 0.75
- variate_bias: float32 [2, 16], P(None, 'tp'), may hold values from -2 to 2
- attn_gain: float32 [1024], replicated, may hold values from 0.25 to 1.75
- ffn_gain: float32 [1024], replicated, may hold values from 0.25 to 1.75
- gate_up: bfloat16 [1024, 64, 128], P(None, ('seq', 'tp')), may hold values from -0.1875 to 0.1875
- w_down: bfloat16 [64, 64, 1024], P(('seq', 'tp')), may hold values from -0.09375 to 0.09375
- cache_keys: bfloat16 [1536, 256, 1024], P(('req', 'seq'), None, 'tp'), may hold values from -360 to 360
- cache_values: bfloat16 [1536, 256, 1024], P(('req', 'seq'), None, 'tp'), may hold values from -6 to 6
- cache_variate: int32 [1536, 256], P(('req', 'seq')), may hold values from 0 to 3
- new_variate: int32 [512, 4], P('req'), may hold values from 0 to 3
- piece_slot: int32 [512, 64], P('req'), may hold values from -1 to 191, as said below
- cache_len: int32 [512], P('req'), may hold values from 1 to 16384, as said below
Outputs:
- layer_out: bfloat16 [2048, 1024], P(('req', 'seq', 'tp'))
Inputs may be any that keep to these rules, and one draw needn't show every extreme that they name: `cache_len`: in each aligned block of 64 requests exactly one request has the most cached positions. `piece_slot`: entry p of request r is the slot within its group that holds cache positions p * 256 to p * 256 + 255; it is -1 exactly when p * 256 >= cache_len[r]; no slot of a group holds two pieces; slots that hold no piece are never read.
All inputs are finite; a program needn't handle non-finite values.
Results may differ from a plain program's by a relative error of at most 0.022.
Values may be sent and summed in bfloat16 or wider, within the bound.
No kernel may reach another device: no remote copies, remote signals or barrier semaphores. Data moves between devices by JAX's collectives and lax.ppermute only.
A program may use at most 64 MiB of HBM per device.

v0:
```python
import math
import jax
import jax.numpy as jnp
from jax import lax
from jax.sharding import PartitionSpec as P

HD = 64
EPSILON = 1e-05
MASKED_SCORE = -1e30


def joined(value, axis, combine):
    everything = jax.tree.map(lambda part: lax.all_gather(part, axis), value)
    first = jax.tree.map(lambda part: part[0], everything)

    def step(k, so_far):
        return combine(so_far, jax.tree.map(lambda part: part[k], everything))

    return lax.fori_loop(1, lax.axis_size(axis), step, first)


def rms_scale(rows, gain):
    rows32 = rows.astype(jnp.float32)
    mean_sq = jnp.mean(rows32 * rows32, axis=-1, keepdims=True)
    return (rows32 * lax.rsqrt(mean_sq + EPSILON) * gain).astype(jnp.bfloat16)


def rotate(vectors, positions):
    half_size = vectors.shape[-1] // 2
    inv_freq = 10000.0 ** (-jnp.arange(half_size, dtype=jnp.float32) / half_size)
    angles = positions[:, None] * inv_freq[None, :]
    cosine = jnp.cos(angles)[:, None, :]
    sine_part = jnp.sin(angles)[:, None, :]
    earlier = vectors[..., :half_size]
    latter = vectors[..., half_size:]
    return jnp.concatenate(
        [earlier * cosine - latter * sine_part, latter * cosine + earlier * sine_part], axis=-1
    )


def row_positions(lengths, step_count):
    offsets = jnp.arange(step_count, dtype=jnp.int32)
    return (lengths[:, None] + offsets[None, :]).reshape(-1).astype(jnp.float32)


def split_heads(projected, positions, head_size):
    row_count = projected.shape[0]
    parts = projected.reshape(row_count, 3, -1, head_size)
    queries = rotate(parts[:, 0], positions).astype(jnp.bfloat16)
    keys_new = rotate(parts[:, 1], positions).astype(jnp.bfloat16)
    values_new = parts[:, 2].astype(jnp.bfloat16)
    return (queries, keys_new, values_new)


def cache_partials(
    queries,
    cache_keys,
    cache_values,
    cache_variate,
    new_variate,
    piece_slot,
    cache_len,
    variate_bias,
    score_scale,
):
    slot_count, piece_len, _ = cache_keys.shape
    requests, step_count, heads, head_size = queries.shape
    max_pieces = piece_slot.shape[1]
    slot_ids = lax.axis_index("seq") * slot_count + jnp.arange(slot_count, dtype=jnp.int32)
    matches = piece_slot[None, :, :] == slot_ids[:, None, None]
    owners = jnp.any(matches, axis=2)
    piece_index = jnp.sum(
        jnp.where(matches, jnp.arange(max_pieces, dtype=jnp.int32)[None, None, :], 0), axis=(1, 2)
    )
    owner_len = jnp.sum(jnp.where(owners, cache_len[None, :], 0), axis=1)
    positions_in = (
        piece_index[:, None] * piece_len + jnp.arange(piece_len, dtype=jnp.int32)[None, :]
    )
    is_valid = positions_in < owner_len[:, None]
    picker = owners.astype(jnp.bfloat16)
    slot_query = jnp.dot(
        picker, queries.reshape(requests, -1), preferred_element_type=jnp.float32
    ).astype(jnp.bfloat16)
    slot_query = slot_query.reshape(slot_count, step_count, heads, head_size)
    slot_variate = jnp.sum(jnp.where(owners[:, :, None], new_variate[None], 0), axis=1)
    same_var = slot_variate[:, :, None] == cache_variate[:, None, :]
    bias_terms = jnp.where(
        same_var[:, None],
        variate_bias[0][None, :, None, None],
        variate_bias[1][None, :, None, None],
    )
    key_rows = cache_keys.reshape(slot_count, piece_len, heads, head_size)
    value_rows = cache_values.reshape(slot_count, piece_len, heads, head_size)
    scores = (
        jnp.einsum("sthd,slhd->shtl", slot_query, key_rows, preferred_element_type=jnp.float32)
        * score_scale
        + bias_terms
    )
    scores = jnp.where(is_valid[:, None, None, :], scores, MASKED_SCORE)
    slot_top = jnp.max(scores, axis=3)
    weights = jnp.where(is_valid[:, None, None, :], jnp.exp(scores - slot_top[..., None]), 0.0)
    slot_total = jnp.sum(weights, axis=3)
    slot_out = jnp.einsum(
        "shtl,slhd->shtd",
        weights.astype(jnp.bfloat16),
        value_rows,
        preferred_element_type=jnp.float32,
    )
    top_cache = jnp.max(
        jnp.where(owners[:, :, None, None], slot_top[:, None], MASKED_SCORE), axis=0
    )
    top_at = jnp.sum(jnp.where(owners[:, :, None, None], top_cache[None], 0.0), axis=1)
    factor = jnp.exp(slot_top - top_at)
    owner_f = owners.astype(jnp.float32)
    cache_total = jnp.einsum(
        "sr,sht->rht", owner_f, slot_total * factor, precision=lax.Precision.HIGHEST
    )
    cache_out = jnp.einsum(
        "sr,shtd->rhtd", owner_f, slot_out * factor[..., None], precision=lax.Precision.HIGHEST
    )
    return (top_cache, cache_total, cache_out)


def merge_pair(earlier, latter):
    joint_top = jnp.maximum(earlier[0], latter[0])
    left_scale = jnp.exp(earlier[0] - joint_top)
    right_scale = jnp.exp(latter[0] - joint_top)
    joint_total = earlier[1] * left_scale + latter[1] * right_scale
    joint_out = earlier[2] * left_scale[..., None] + latter[2] * right_scale[..., None]
    return (joint_top, joint_total, joint_out)


def finish(
    top_cache,
    cache_total,
    cache_out,
    queries,
    keys_new,
    values_new,
    new_variate,
    variate_bias,
    score_scale,
):
    step_count = new_variate.shape[1]
    new_scores = (
        jnp.einsum("rthd,ruhd->rhtu", queries, keys_new, preferred_element_type=jnp.float32)
        * score_scale
    )
    same_var = new_variate[:, :, None] == new_variate[:, None, :]
    new_scores = new_scores + jnp.where(
        same_var[:, None],
        variate_bias[0][None, :, None, None],
        variate_bias[1][None, :, None, None],
    )
    step_ids = jnp.arange(step_count, dtype=jnp.int32)
    causal = step_ids[:, None] >= step_ids[None, :]
    new_scores = jnp.where(causal[None, None], new_scores, MASKED_SCORE)
    row_top = jnp.maximum(top_cache, jnp.max(new_scores, axis=3))
    new_weights = jnp.where(causal[None, None], jnp.exp(new_scores - row_top[..., None]), 0.0)
    carried = jnp.exp(top_cache - row_top)
    row_total = cache_total * carried + jnp.sum(new_weights, axis=3)
    mixed_out = cache_out * carried[..., None] + jnp.einsum(
        "rhtu,ruhd->rhtd",
        new_weights.astype(jnp.bfloat16),
        values_new,
        preferred_element_type=jnp.float32,
    )
    attended = mixed_out / row_total[..., None]
    requests, heads, _, head_size = attended.shape
    return (
        jnp.transpose(attended, (0, 2, 1, 3))
        .reshape(requests * step_count, heads * head_size)
        .astype(jnp.bfloat16)
    )


def make_expand(gate_blocks, unit_block, row_block):
    block_count = gate_blocks.shape[1]
    expanded = jnp.einsum("nd,dbu->nbu", row_block, gate_blocks, preferred_element_type=jnp.float32)
    gate_part = expanded[:, :, :unit_block]
    up_part = expanded[:, :, unit_block:]
    return (
        (jax.nn.silu(gate_part) * up_part)
        .astype(jnp.bfloat16)
        .reshape(row_block.shape[0], block_count * unit_block)
    )


def on_device(
    tokens,
    w_qkv,
    w_out,
    variate_bias,
    attn_gain,
    ffn_gain,
    gate_up,
    w_down,
    cache_keys,
    cache_values,
    cache_variate,
    new_variate,
    piece_slot,
    cache_len,
):
    row_count = tokens.shape[0]
    requests, step_count = new_variate.shape
    score_scale = 1.0 / math.sqrt(HD)
    normed = rms_scale(tokens, attn_gain)
    qkv_width = w_qkv.shape[2]
    flat_qkv = w_qkv.reshape(w_qkv.shape[0], 3 * qkv_width)
    projected = jnp.dot(
        lax.all_gather(normed, ("seq", "tp"), axis=0, tiled=True),
        flat_qkv,
        preferred_element_type=jnp.float32,
    )
    queries, keys_new, values_new = split_heads(projected, row_positions(cache_len, step_count), HD)
    shape_four = (requests, step_count, qkv_width // HD, HD)
    queries = queries.reshape(shape_four)
    keys_new = keys_new.reshape(shape_four)
    values_new = values_new.reshape(shape_four)
    top_cache, cache_total, cache_out = cache_partials(
        queries,
        cache_keys,
        cache_values,
        cache_variate,
        new_variate,
        piece_slot,
        cache_len,
        variate_bias,
        score_scale,
    )
    top_cache, cache_total, cache_out = joined(
        (top_cache, cache_total, cache_out), "seq", merge_pair
    )
    attended = finish(
        top_cache,
        cache_total,
        cache_out,
        queries,
        keys_new,
        values_new,
        new_variate,
        variate_bias,
        score_scale,
    )
    seq_base = lax.axis_index("seq") * (row_count * lax.axis_size("tp"))
    picked = lax.dynamic_slice_in_dim(attended, seq_base, row_count * lax.axis_size("tp"), 0)
    attn_rows_sum = lax.psum_scatter(
        jnp.dot(picked, w_out, preferred_element_type=jnp.float32).astype(jnp.bfloat16),
        "tp",
        scatter_dimension=0,
        tiled=True,
    ).astype(jnp.float32)
    mid = tokens.astype(jnp.float32) + attn_rows_sum
    normed_mid = rms_scale(mid, ffn_gain)
    unit_block = w_down.shape[1]
    model_width = w_down.shape[2]
    hidden = make_expand(
        gate_up, unit_block, lax.all_gather(normed_mid, ("seq", "tp"), axis=0, tiled=True)
    )
    flat_down = w_down.reshape(w_down.shape[0] * unit_block, model_width)
    picked = hidden
    ffn_rows_sum = lax.psum_scatter(
        jnp.dot(picked, flat_down, preferred_element_type=jnp.float32),
        ("seq", "tp"),
        scatter_dimension=0,
        tiled=True,
    )
    return (mid + ffn_rows_sum).astype(jnp.bfloat16)


def solution(mesh):
    in_specs = (
        P(("req", "seq", "tp"), None),
        P(None, None, "tp"),
        P("tp", None),
        P(None, "tp"),
        P(),
        P(),
        P(None, ("seq", "tp"), None),
        P(("seq", "tp"), None, None),
        P(("req", "seq"), None, "tp"),
        P(("req", "seq"), None, "tp"),
        P(("req", "seq"), None),
        P("req", None),
        P("req", None),
        P("req"),
    )
    out_specs = P(("req", "seq", "tp"), None)
    return jax.shard_map(
        on_device, mesh=mesh, in_specs=in_specs, out_specs=out_specs, check_vma=False
    )
```

profile of v0, /device:TPU:8, one launch (start us, length us, event | category | flops | bytes accessed | tf_op | source)
XLA Modules:
  0.0 463.1 jit_solution(17933760203444792327)
XLA Ops:
  6.6 1.4 fusion.9
  8.0 1.3 compare_reduce_fusion
  9.9 0.8 fusion.31
  10.8 1.3 slice_bitcast_fusion.3
  12.1 0.7 add_convert_fusion.2
  12.8 1.3 select_reduce_fusion.3
  14.1 0.8 select_reduce_fusion.2
  14.9 0.7 copy.148
  15.7 0.8 fusion.39
  16.5 55.1 %all-gather.3 = bf16[64,4,1024]{2,1,0:T(4,128)(2,1)S(1)} all-gather(bf16[1,4,1024]{2,1,0:T(4,128)(2,1)S(1)} %fusion.39), channel_id=1, replica_groups=mesh['req'=8,'seq'=8,'tp'=8] {'seq','tp'}, dimensions={0}, use_global_device_ids=true | all-gather | bytes 532480 | tf_op jit(solution)/shard_map/all_gather | solution.py:212
  72.4 0.8 copy-done.3
  73.4 0.7 subtract_convert_fusion.1
  74.6 0.7 copy.146
  75.4 0.9 broadcast_compare_fusion
  76.4 1.7 fusion.47
  78.3 1.2 fusion.20
  79.8 0.7 copy.154
  80.5 1.5 convolution_multiply_fusion.1
  82.0 1.0 fusion.22
  83.1 0.9 slice.97
  85.9 13.5 %all-gather = f32[512,2,4]{2,1,0:T(2,128)S(1)} all-gather(f32[64,2,4]{2,1,0:T(2,128)S(1)} %copy.150), channel_id=2, replica_groups=mesh['req'=8,'seq'=8,'tp'=8] {'seq'}, dimensions={0}, use_global_device_ids=true | all-gather | bytes 18432 | tf_op jit(solution)/shard_map/all_gather | solution.py:13
  99.7 13.6 %all-gather.1 = f32[512,2,4]{2,1,0:T(2,128)S(1)} all-gather(f32[64,2,4]{2,1,0:T(2,128)S(1)} %copy.153), channel_id=3, replica_groups=mesh['req'=8,'seq'=8,'tp'=8] {'seq'}, dimensions={0}, use_global_device_ids=true | all-gather | bytes 18432 | tf_op jit(solution)/shard_map/all_gather | solution.py:13
  113.8 1.0 slice.67
  114.9 14.4 %while.19 = (s32[]{:T(128)}, f32[64,2,4]{0,2,1:T(4,128)S(1)}, f32[64,2,4]{0,2,1:T(4,128)S(1)}, f32[64,2,4,64]{3,2,1,0:T(4,128)S(1)}, f32[8,64,2,4]{1,3,2,0:T(4,1...) while((s32[]{:T(128)}, f32[64,2,4]{0,2,1:T(4,128)S(1)}, ...), condition=%wide.region_10.11_spmd, body=%wide.region_9.10_spmd.sunk | while | flops 101381 | bytes 684175 | solution.py:19
  115.2 1.0 constant_dynamic-slice_fusion.2
  116.2 0.8 fusion.62
  117.3 1.0 constant_dynamic-slice_fusion.2
  118.3 0.8 fusion.62
  119.4 1.0 constant_dynamic-slice_fusion.2
  120.3 0.8 fusion.62
  121.4 1.0 constant_dynamic-slice_fusion.2
  122.4 0.8 fusion.62
  123.5 1.0 constant_dynamic-slice_fusion.2
  124.5 0.8 fusion.62
  125.5 1.0 constant_dynamic-slice_fusion.2
  126.5 0.8 fusion.62
  127.6 1.0 constant_dynamic-slice_fusion.2
  128.6 0.8 fusion.62
  130.6 0.8 convolution_convert_fusion
  131.5 1.3 dynamic-slice
  133.4 74.0 %all-reduce.5.cloned.1.call-done = bf16[32,1024]{1,0:T(8,128)(2,1)} async-done(((bf16[32,1024]{1,0:T(8,128)(2,1)}), bf16[32,1024]{1,0:T(8,128)(2,1)}) %all-reduce.5.cloned.1.call-update) | async-done | bytes 65552
  207.4 0.8 multiply_reduce_fusion
  208.2 0.8 fusion.38
  209.0 48.0 %all-gather.4 = bf16[64,4,1024]{2,1,0:T(4,128)(2,1)S(1)} all-gather(bf16[1,4,1024]{2,1,0:T(4,128)(2,1)S(1)} %fusion.38), channel_id=1, replica_groups=mesh['req'=8,'seq'=8,'tp'=8] {'seq','tp'}, dimensions={0}, use_global_device_ids=true | all-gather | bytes 532480 | tf_op jit(solution)/shard_map/all_gather | solution.py:259
  257.5 1.4 fusion.13
  258.9 1.3 dynamic-slice.2
  260.8 194.3 %all-reduce.7.cloned.1.call-done = f32[256,1024]{1,0:T(8,128)} async-done(((f32[256,1024]{1,0:T(8,128)}), f32[256,1024]{1,0:T(8,128)}) %all-reduce.7.cloned.1.call-update) | async-done | bytes 1048592
  455.2 1.4 fusion.34
  (118 shorter events, 9.1 us)
Async XLA Ops:
  6.5 124.0 %copy-start = (bf16[128,1024]{1,0:T(8,128)(2,1)S(1)}, bf16[128,1024]{1,0:T(8,128)(2,1)}, u32[]{:S(2)}) copy-start(bf16[128,1024]{1,0:T(8,128)(2,1)} %param.18) | copy-start | bytes 786436
  6.5 65.1 %copy-start.4 = (bf16[1024,3,128]{2,0,1:T(8,128)(2,1)S(1)}, bf16[1024,3,128]{2,0,1:T(8,128)(2,1)}, u32[]{:S(2)}) copy-start(bf16[1024,3,128]{2,0,1:T(8,128)(2,1)} %param.17) | copy-start | bytes 2359300
  6.5 107.2 %all-gather.7.cloned.1.call-start = ((), (), s32[]{:S(2)}) async-start(), calls=%async_computation | async-start | bytes 2359296 | tf_op jit(solution)/shard_map/all_gather | solution.py:13
  72.0 2.6 copy-start.1
  72.4 0.8 copy-start.3
  74.5 0.7 copy-start.16
  74.6 0.7 copy-start.17
  74.6 0.8 copy-start.12
  75.3 4.4 copy-start.2
  75.4 2.6 copy-start.10
  79.7 0.7 copy-start.11
  80.5 4.1 copy-start.8
  80.5 4.2 copy-start.7
  83.1 124.3 %all-reduce.5.cloned.1.call-start = ((), (), s32[]{:S(2)}) async-start(), calls=%async_computation.1 | async-start | bytes 131072
  85.5 28.2 %copy-start.13 = (s32[64,4]{0,1:T(4,128)S(1)}, s32[64,4]{0,1:T(4,128)}, u32[]{:S(2)}) copy-start(s32[64,4]{0,1:T(4,128)} %param.27) | copy-start | bytes 3076
  85.5 28.2 %copy-start.14 = (f32[2]{0:T(128)S(1)}, f32[2]{0:T(128)}, u32[]{:S(2)}) copy-start(f32[2]{0:T(128)} %get-tuple-element.258) | copy-start | bytes 28
  129.9 77.5 %copy-start.6 = (bf16[4,1024]{1,0:T(4,128)(2,1)S(1)}, bf16[4,1024]{1,0:T(4,128)(2,1)}, u32[]{:S(2)}) copy-start(bf16[4,1024]{1,0:T(4,128)(2,1)} %param.16) | copy-start | bytes 24580
  129.9 78.3 %copy-start.15 = (f32[1024]{0:T(1024)S(1)}, f32[1024]{0:T(1024)}, u32[]{:S(2)}) copy-start(f32[1024]{0:T(1024)} %param.21) | copy-start | bytes 12292
  130.3 126.9 %copy-start.5 = (bf16[1024,1,128]{2,0,1:T(8,128)(2,1)S(1)}, bf16[1024,1,128]{2,0,1:T(8,128)(2,1)}, u32[]{:S(2)}) copy-start(bf16[1024,1,128]{2,0,1:T(8,128)(2,1)} %param.22) | copy-start | bytes 786436
  130.4 127.1 %copy-start.9 = (bf16[1,64,1024]{2,1,0:T(8,128)(2,1)S(1)}, bf16[1,64,1024]{2,1,0:T(8,128)(2,1)}, u32[]{:S(2)}) copy-start(bf16[1,64,1024]{2,1,0:T(8,128)(2,1)} %param.23) | copy-start | bytes 393220
  131.4 323.8 %all-reduce.7.cloned.1.call-start = ((), (), s32[]{:S(2)}) async-start(), calls=%async_computation.2 | async-start | bytes 2097152
Sparse Core Ops, SparseCore 0:
  83.2 27.9 all-gather.6
  131.5 75.8 all-reduce.4
  259.0 196.1 all-reduce.6
where the time goes:
time: 464 us; the launch traced here: 463 us
  waiting for transfers between devices  268 us (58%)
  blocking collectives  130 us (28%)
  local copies, waits for them, and re-layouts  20.9 us (5%)
  other arithmetic  20.4 us (4%)
  between operations  14.9 us (3%)
  matrix products  7.98 us (2%)
    unnamed x5, waiting for transfers between devices  268 us
    all_gather x1, blocking collectives, on_device(): lax.all_gather(normed, ('seq', 'tp'), axis=0, tiled=True)  55.1 us
    all_gather x1, blocking collectives, on_device(): lax.all_gather(normed_mid, ('seq', 'tp'), axis=0, tiled=True)  48 us
    all_gather x2, blocking collectives, joined(): everything = jax.tree.map(lambda part: lax.all_gather(part, axis), value)  27.1 us
  transfers between devices with their start and end apart: 3, of which 2 were waited for; matrix products, arithmetic and copies ran while one was open for 1% of the time, Pallas kernels for 0%

commit v1 on v0

--- a/solution.py
+++ b/solution.py
@@ -7,6 +7,11 @@
 HD = 64
 EPSILON = 1e-05
 MASKED_SCORE = -1e30
+
+
+def gather_by_exchange(x, axis, dim):
+    copies = jnp.concatenate([x] * lax.axis_size(axis), axis=dim)
+    return lax.all_to_all(copies, axis, dim, dim, tiled=True)
 
 
 def joined(value, axis, combine):
@@ -209,9 +214,7 @@
     qkv_width = w_qkv.shape[2]
     flat_qkv = w_qkv.reshape(w_qkv.shape[0], 3 * qkv_width)
     projected = jnp.dot(
-        lax.all_gather(normed, ("seq", "tp"), axis=0, tiled=True),
-        flat_qkv,
-        preferred_element_type=jnp.float32,
+        gather_by_exchange(normed, ("seq", "tp"), 0), flat_qkv, preferred_element_type=jnp.float32
     )
     queries, keys_new, values_new = split_heads(projected, row_positions(cache_len, step_count), HD)
     shape_four = (requests, step_count, qkv_width // HD, HD)

time: 464 us -> 437 us (0.942)
  blocking collectives: 130 us -> 75.2 us
  starting transfers between devices: 0.09 us -> 13.9 us
  waiting for transfers between devices: 268 us -> 278 us
  local copies, waits for them, and re-layouts: 20.9 us -> 27.3 us
    all_gather x1 -> x0, blocking collectives: 55.1 us -> none  [on_device(): lax.all_gather(normed, ('seq', 'tp'), axis=0, tiled=True)]
    all_to_all x0 -> x1, starting transfers between devices: none -> 13.8 us  [gather_by_exchange(): return lax.all_to_all(copies, axis, dim, dim, tiled=True)]
    all_to_all x0 -> x1, waiting for transfers between devices: none -> 10 us  [gather_by_exchange(): return lax.all_to_all(copies, axis, dim, dim, tiled=True)]
  transfers between devices with their start and end apart: 3 -> 4, of which waited for: 2 -> 3; matrix products, arithmetic and copies ran while one was open for 1% -> 3% of each run, Pallas kernels for 0% -> 0%
where the time goes in v1:
time: 437 us; the launch traced here: 436 us
  waiting for transfers between devices  278 us (64%)
  blocking collectives  75.2 us (17%)
  local copies, waits for them, and re-layouts  27.3 us (6%)
  other arithmetic  16.2 us (4%)
  between operations  14.9 us (3%)
  starting transfers between devices  13.9 us (3%)
  matrix products  9.99 us (2%)
    unnamed x5, waiting for transfers between devices  268 us
    all_gather x1, blocking collectives, on_device(): lax.all_gather(normed_mid, ('seq', 'tp'), axis=0, tiled=True)  48 us
    all_gather x2, blocking collectives, joined(): everything = jax.tree.map(lambda part: lax.all_gather(part, axis), value)  27.2 us
    all_to_all x1, starting transfers between devices, gather_by_exchange(): return lax.all_to_all(copies, axis, dim, dim, tiled=True)  13.8 us
    all_to_all x1, waiting for transfers between devices, gather_by_exchange(): return lax.all_to_all(copies, axis, dim, dim, tiled=True)  10 us
  transfers between devices with their start and end apart: 4, of which 3 were waited for; matrix products, arithmetic and copies ran while one was open for 3% of the time, Pallas kernels for 0%

profile of v1, /device:TPU:8, one launch (start us, length us, event | category | flops | bytes accessed | tf_op | source)
XLA Modules:
  0.0 435.5 jit_solution(8810666644449950414)
XLA Ops:
  6.5 0.9 fusion.31
  7.4 0.8 fusion.33
  8.2 1.0 concatenate.24
  9.3 1.0 all_to_all.8
  10.3 13.8 %all-to-all-start = ((bf16[64,4,1024]{2,1,0:T(4,128)(2,1)}), bf16[64,4,1024]{2,1,0:T(4,128)(2,1)S(1)}, u32[]{:S(2)}, u32[]{:S(2)}) async-start(bf16[64,4,1024]{2,1,0:T(4,128)(2,1)} %all_to_all.8), calls=%async_computation | async-start | bytes 1048576 | tf_op jit(solution)/shard_map/all_to_all | solution.py:14
  26.1 1.7 copy.146
  27.8 2.6 copy.154
  31.2 0.7 broadcast_compare_fusion
  32.1 10.0 %all-to-all-done = bf16[64,4,1024]{2,1,0:T(4,128)(2,1)S(1)} async-done(((bf16[64,4,1024]{2,1,0:T(4,128)(2,1)}), bf16[64,4,1024]{2,1,0:T(4,128)(2,1)S(1)}, u32[]{:S(2)}, u32[]{:S(2)}) %all-to-all-start) | async-done | bytes 524320 | tf_op jit(solution)/shard_map/all_to_all | solution.py:14
  42.1 0.9 reshape.224
  43.0 1.4 fusion.10
  44.5 0.7 copy-done.2
  47.1 1.0 copy.145
  48.1 0.8 convert_element_type.69
  48.9 1.0 convolution_convert_fusion.1
  49.9 1.8 fusion.46
  52.1 1.2 fusion.20
  53.5 1.5 convolution_multiply_fusion.1
  55.0 1.0 fusion.22
  56.2 0.9 slice.97
  58.9 13.4 %all-gather = f32[512,2,4]{2,1,0:T(2,128)S(1)} all-gather(f32[64,2,4]{2,1,0:T(2,128)S(1)} %copy.150), channel_id=2, replica_groups=mesh['req'=8,'seq'=8,'tp'=8] {'seq'}, dimensions={0}, use_global_device_ids=true | all-gather | bytes 18432 | tf_op jit(solution)/shard_map/all_gather | solution.py:18
  72.7 13.7 %all-gather.1 = f32[512,2,4]{2,1,0:T(2,128)S(1)} all-gather(f32[64,2,4]{2,1,0:T(2,128)S(1)} %copy.153), channel_id=3, replica_groups=mesh['req'=8,'seq'=8,'tp'=8] {'seq'}, dimensions={0}, use_global_device_ids=true | all-gather | bytes 18432 | tf_op jit(solution)/shard_map/all_gather | solution.py:18
  86.9 1.0 slice.67
  88.1 14.4 %while.19 = (s32[]{:T(128)}, f32[64,2,4]{0,2,1:T(4,128)S(1)}, f32[64,2,4]{0,2,1:T(4,128)S(1)}, f32[64,2,4,64]{3,2,1,0:T(4,128)S(1)}, f32[8,64,2,4]{1,3,2,0:T(4,1...) while((s32[]{:T(128)}, f32[64,2,4]{0,2,1:T(4,128)S(1)}, ...), condition=%wide.region_10.11_spmd, body=%wide.region_9.10_spmd.sunk | while | flops 101381 | bytes 684175 | solution.py:24
  88.3 1.0 constant_dynamic-slice_fusion.2
  89.3 0.8 fusion.61
  90.4 1.0 constant_dynamic-slice_fusion.2
  91.4 0.8 fusion.61
  92.5 1.0 constant_dynamic-slice_fusion.2
  93.4 0.8 fusion.61
  94.5 1.0 constant_dynamic-slice_fusion.2
  95.5 0.8 fusion.61
  96.6 1.0 constant_dynamic-slice_fusion.2
  97.6 0.8 fusion.61
  98.6 1.0 constant_dynamic-slice_fusion.2
  99.6 0.8 fusion.61
  100.7 1.0 constant_dynamic-slice_fusion.2
  101.7 0.8 fusion.61
  103.7 0.8 convolution_convert_fusion
  104.6 1.3 dynamic-slice
  106.5 73.2 %all-reduce.5.cloned.1.call-done = bf16[32,1024]{1,0:T(8,128)(2,1)} async-done(((bf16[32,1024]{1,0:T(8,128)(2,1)}), bf16[32,1024]{1,0:T(8,128)(2,1)}) %all-reduce.5.cloned.1.call-update) | async-done | bytes 65552
  179.7 0.8 multiply_reduce_fusion
  180.5 0.8 fusion.38
  181.3 48.0 %all-gather.3 = bf16[64,4,1024]{2,1,0:T(4,128)(2,1)S(1)} all-gather(bf16[1,4,1024]{2,1,0:T(4,128)(2,1)S(1)} %fusion.38), channel_id=1, replica_groups=mesh['req'=8,'seq'=8,'tp'=8] {'seq','tp'}, dimensions={0}, use_global_device_ids=true | all-gather | bytes 532480 | tf_op jit(solution)/shard_map/all_gather | solution.py:262
  229.8 1.4 fusion.13
  231.2 1.3 dynamic-slice.2
  233.1 194.5 %all-reduce.7.cloned.1.call-done = f32[256,1024]{1,0:T(8,128)} async-done(((f32[256,1024]{1,0:T(8,128)}), f32[256,1024]{1,0:T(8,128)}) %all-reduce.7.cloned.1.call-update) | async-done | bytes 1048592
  427.6 1.4 fusion.34
  (127 shorter events, 11.7 us)
Async XLA Ops:
  6.5 97.1 %copy-start = (bf16[128,1024]{1,0:T(8,128)(2,1)S(1)}, bf16[128,1024]{1,0:T(8,128)(2,1)}, u32[]{:S(2)}) copy-start(bf16[128,1024]{1,0:T(8,128)(2,1)} %param.18) | copy-start | bytes 786436
  8.2 15.9 %copy-start.13 = (s32[64,64]{1,0:T(8,128)S(1)}, s32[64,64]{1,0:T(8,128)}, u32[]{:S(2)}) copy-start(s32[64,64]{1,0:T(8,128)} %param.28) | copy-start | bytes 49156
  8.2 17.1 %copy-start.19 = (s32[64]{0:T(128)S(1)}, s32[64]{0:T(128)}, u32[]{:S(2)}) copy-start(s32[64]{0:T(128)} %param.29) | copy-start | bytes 772
  8.2 17.2 %copy-start.15 = (s32[64,4]{0,1:T(4,128)S(1)}, s32[64,4]{0,1:T(4,128)}, u32[]{:S(2)}) copy-start(s32[64,4]{0,1:T(4,128)} %param.27) | copy-start | bytes 3076
  8.2 17.5 %copy-start.3 = (bf16[1024,3,128]{2,0,1:T(8,128)(2,1)S(1)}, bf16[1024,3,128]{2,0,1:T(8,128)(2,1)}, u32[]{:S(2)}) copy-start(bf16[1024,3,128]{2,0,1:T(8,128)(2,1)} %param.17) | copy-start | bytes 2359300
  10.3 31.8 %all-to-all-start = ((bf16[64,4,1024]{2,1,0:T(4,128)(2,1)}), bf16[64,4,1024]{2,1,0:T(4,128)(2,1)S(1)}, u32[]{:S(2)}, u32[]{:S(2)}) async-start(bf16[64,4,1024]{2,1,0:T(4,128)(2,1)} %all_to_all.8), calls=%async_computation | async-start | bytes 1048576 | tf_op jit(solution)/shard_map/all_to_all | solution.py:14
  24.1 62.8 %all-gather.6.cloned.1.call-start = ((), (), s32[]{:S(2)}) async-start(), calls=%async_computation.1 | async-start | bytes 2359296 | tf_op jit(solution)/shard_map/all_gather | solution.py:18
  27.8 2.7 copy-start.20
  27.8 3.4 copy-start.14
  44.5 0.7 copy-start.2
  45.9 0.6 copy-start.4
  45.9 0.6 copy-start.6
  45.9 7.5 %copy-start.1 = (bf16[24,256,128]{1,2,0:T(8,128)(2,1)S(1)}, bf16[24,256,128]{1,2,0:T(8,128)(2,1)}, u32[]{:S(2)}) copy-start(bf16[24,256,128]{1,2,0:T(8,128)(2,1)} %copy.154) | copy-start | bytes 4718596
  53.5 3.6 copy-start.7
  53.5 3.7 copy-start.5
  53.5 4.1 copy-start.11
  53.5 4.2 copy-start.10
  56.1 123.6 %all-reduce.5.cloned.1.call-start = ((), (), s32[]{:S(2)}) async-start(), calls=%async_computation.2 | async-start | bytes 131072
  58.5 28.2 %copy-start.16 = (f32[2]{0:T(128)S(1)}, f32[2]{0:T(128)}, u32[]{:S(2)}) copy-start(f32[2]{0:T(128)} %get-tuple-element.257) | copy-start | bytes 28
  58.5 28.2 %copy-start.17 = (f32[2]{0:T(128)S(1)}, f32[2]{0:T(128)}, u32[]{:S(2)}) copy-start(f32[2]{0:T(128)} %get-tuple-element.258) | copy-start | bytes 28
  103.0 76.6 %copy-start.9 = (bf16[4,1024]{1,0:T(4,128)(2,1)S(1)}, bf16[4,1024]{1,0:T(4,128)(2,1)}, u32[]{:S(2)}) copy-start(bf16[4,1024]{1,0:T(4,128)(2,1)} %param.16) | copy-start | bytes 24580
  103.0 77.5 %copy-start.18 = (f32[1024]{0:T(1024)S(1)}, f32[1024]{0:T(1024)}, u32[]{:S(2)}) copy-start(f32[1024]{0:T(1024)} %param.21) | copy-start | bytes 12292
  103.4 126.0 %copy-start.8 = (bf16[1024,1,128]{2,0,1:T(8,128)(2,1)S(1)}, bf16[1024,1,128]{2,0,1:T(8,128)(2,1)}, u32[]{:S(2)}) copy-start(bf16[1024,1,128]{2,0,1:T(8,128)(2,1)} %param.22) | copy-start | bytes 786436
  103.5 126.2 %copy-start.12 = (bf16[1,64,1024]{2,1,0:T(8,128)(2,1)S(1)}, bf16[1,64,1024]{2,1,0:T(8,128)(2,1)}, u32[]{:S(2)}) copy-start(bf16[1,64,1024]{2,1,0:T(8,128)(2,1)} %param.23) | copy-start | bytes 393220
  104.5 323.1 %all-reduce.7.cloned.1.call-start = ((), (), s32[]{:S(2)}) async-start(), calls=%async_computation.3 | async-start | bytes 2097152
Sparse Core Ops, SparseCore 0:
  56.2 27.3 all-gather.5
  104.6 74.9 all-reduce.4
  231.3 196.2 all-reduce.6
